TPU v7x, 32 devices: a whole 2x2x4 slice. The times are simulated.
32 devices in a mesh: req: 8 (over z, x), head: 4 (over y, core).
Axes of the slice: x: 2, y: 2, z: 4, core: 2. Of those that a mesh axis runs over, the one named last changes fastest.
Arguments:
- residual_in: bfloat16 [1024, 1536], P(('req', 'head')), may hold values from -3 to 3
- attn_gain: bfloat16 [1536], replicated, may hold values from 0.099609375 to 1.8984375
- w_qkv: bfloat16 [1536, 8, 320], P(None, 'head'), may hold values from -0.15625 to 0.15625
- w_out: bfloat16 [1536, 1536], P('head'), may hold values from -0.41992188 to 0.41992188
- kv_cache: bfloat16 [1024, 8, 192, 128], P('req', 'head'), as said below
- lengths: int32 [1024], P('req'), may hold values from 1 to 192, as said below
- moe_gain: bfloat16 [1536], replicated, may hold values from 0.099609375 to 1.8984375
- w_router: bfloat16 [1536, 24], replicated
- routes: int32 [1024, 8], P(('req', 'head')), may hold values from 0 to 23, all different within a row; in each aligned block of 32 rows (0 to 31, 32 to 63, ...) at most 12 rows name the same one
- w_in: bfloat16 [24, 1536, 1024], P('req'), may hold values from -0.15625 to 0.15625
- w_down: bfloat16 [24, 512, 1536], P('req'), may hold values from -0.5 to 0.5
Outputs:
- layer_out: bfloat16 [1024, 1536], P(('req', 'head'))
- new_kv: bfloat16 [1024, 8, 128], P('req', 'head')
Inputs may be any that keep to these rules, and one draw needn't show every extreme that they name: `kv_cache`: each position holds its key in the first 64 entries and its value in the last 64. `lengths`: some request has exactly 192 cached positions. `routes`: each row names 8 different experts. Among the 32 rows of one device no expert is named more than 12 times, a bound that some block reaches.
All inputs are finite; a program needn't handle non-finite values.
Results may differ from a plain program's by a relative error of at most 0.017.
Values may be sent and summed in bfloat16 or wider, within the bound.
A program may use at most 128 MiB of HBM per device.

v0:
```python
import jax
import jax.numpy as jnp
from jax import lax
from jax.sharding import PartitionSpec as P

D = 1536
HEADS = 24
KV = 8
HD = 64
F = 512
EPSILON = 1e-06
THETA = 10000.0


def rms_scale(values, gain):
    wide = values.astype(jnp.float32)
    mean_square = jnp.mean(wide * wide, axis=-1, keepdims=True)
    return (wide * lax.rsqrt(mean_square + EPSILON) * gain.astype(jnp.float32)).astype(jnp.bfloat16)


def rotate(vectors, lengths):
    half = vectors.shape[-1] // 2
    index = jnp.arange(half).astype(jnp.float32)
    frequency = jnp.power(THETA, -2.0 * index / vectors.shape[-1])
    angle = lengths.astype(jnp.float32)[:, None] * frequency[None, :]
    cosine = jnp.cos(angle)[:, None, None, :]
    sine = jnp.sin(angle)[:, None, None, :]
    first = vectors[..., :half]
    second = vectors[..., half:]
    return jnp.concatenate(
        [first * cosine - second * sine, second * cosine + first * sine], axis=-1
    )


def project_heads(projected, lengths, group, head_size):
    blocks = projected.reshape(projected.shape[0], -1, group + 2, head_size)
    queries = rotate(blocks[:, :, :group], lengths).astype(jnp.bfloat16)
    new_keys = rotate(blocks[:, :, group : group + 1], lengths).astype(jnp.bfloat16)[:, :, 0]
    new_values = blocks[:, :, group + 1].astype(jnp.bfloat16)
    return (queries, new_keys, new_values)


def own_scores(queries, new_keys):
    product = queries.astype(jnp.float32) * new_keys.astype(jnp.float32)[:, :, None, :]
    return jnp.sum(product, axis=-1) * HD ** (-0.5)


def own_term(own_weight, new_values):
    own_prob = own_weight.astype(jnp.bfloat16).astype(jnp.float32)
    return own_prob[..., None] * new_values.astype(jnp.float32)[:, :, None, :]


def attend_full(queries, new_keys, new_values, cache, lengths):
    scores = jnp.einsum(
        "rkgd,rkld->rkgl", queries, cache[..., :HD], preferred_element_type=jnp.float32
    ) * HD ** (-0.5)
    own = own_scores(queries, new_keys)
    positions = jnp.arange(cache.shape[2])
    live = (positions[None, :] < lengths[:, None])[:, None, None, :]
    masked = jnp.where(live, scores, -1e30)
    peak = jnp.maximum(jnp.max(masked, axis=-1), own)
    weights = jnp.where(live, jnp.exp(masked - peak[..., None]), 0.0)
    own_weight = jnp.exp(own - peak)
    total = jnp.sum(weights, axis=-1) + own_weight
    probabilities = weights.astype(jnp.bfloat16)
    weighted = jnp.einsum(
        "rkgl,rkld->rkgd", probabilities, cache[..., HD:], preferred_element_type=jnp.float32
    )
    weighted = weighted + own_term(own_weight, new_values)
    return (weighted / total[..., None]).astype(jnp.bfloat16)


def local(
    residual_in,
    attn_gain,
    w_qkv,
    w_out,
    kv_cache,
    lengths,
    moe_gain,
    w_router,
    routes,
    w_in,
    w_down,
):
    group = HEADS // KV
    tok_rows = residual_in.shape[0]
    req_rows = lengths.shape[0]
    kv_local = w_qkv.shape[1]
    normed = rms_scale(residual_in, attn_gain)
    flat_weight = w_qkv.reshape(D, kv_local * (group + 2) * HD)
    projected = jnp.dot(
        lax.all_gather(normed, "head", axis=0, tiled=True),
        flat_weight,
        preferred_element_type=jnp.float32,
    )
    queries, new_keys, new_values = project_heads(projected, lengths, group, HD)
    new_kv = jnp.concatenate([new_keys, new_values], axis=-1)
    heads_out = attend_full(queries, new_keys, new_values, kv_cache, lengths)
    local_width = kv_local * group * HD
    attn_heads = heads_out.reshape(req_rows, local_width)
    attention = lax.psum_scatter(
        jnp.dot(attn_heads, w_out, preferred_element_type=jnp.float32).astype(jnp.bfloat16),
        "head",
        scatter_dimension=0,
        tiled=True,
    ).astype(jnp.float32)
    attended = (residual_in.astype(jnp.float32) + attention).astype(jnp.bfloat16)
    normed_moe = rms_scale(attended, moe_gain)
    logits = jnp.dot(normed_moe, w_router, preferred_element_type=jnp.float32)
    gates = jax.nn.softmax(jnp.take_along_axis(logits, routes, axis=1), axis=-1)
    top = routes.shape[1]
    experts_all = w_router.shape[1]
    owners = lax.axis_size("req")
    local_experts = w_in.shape[0]
    capacity = (tok_rows * top + experts_all - 1) // experts_all + 1
    chosen = routes.reshape(tok_rows * top)
    onehot = (chosen[:, None] == jnp.arange(experts_all)[None, :]).astype(jnp.int32)
    earlier = jnp.cumsum(onehot, axis=0) - onehot
    within = jnp.sum(earlier * onehot, axis=1)
    slots = chosen * capacity + within
    placed = (slots[:, None] == jnp.arange(experts_all * capacity)[None, :]).astype(jnp.bfloat16)
    source = jnp.repeat(normed_moe, top, axis=0)
    outgoing = jnp.einsum("ps,pd->sd", placed, source, preferred_element_type=jnp.float32).astype(
        jnp.bfloat16
    )
    outgoing = outgoing.reshape(owners, local_experts, capacity, D)
    both = jnp.einsum(
        "sjcd,jdf->sjcf",
        lax.all_to_all(outgoing, "req", split_axis=0, concat_axis=0, tiled=True),
        w_in,
        preferred_element_type=jnp.float32,
    )
    hidden = (jax.nn.silu(both[..., :F]) * both[..., F:]).astype(jnp.bfloat16)
    result = jnp.einsum(
        "sjcf,jfd->sjcd", hidden, w_down, preferred_element_type=jnp.float32
    ).astype(jnp.bfloat16)
    returned = lax.all_to_all(result, "req", split_axis=0, concat_axis=0, tiled=True)
    picked = jnp.take(returned.reshape(experts_all * capacity, D), slots, axis=0).reshape(
        tok_rows, top, D
    )
    mixed = jnp.sum(gates[:, :, None] * picked.astype(jnp.float32), axis=1)
    layer_out = (attended.astype(jnp.float32) + mixed).astype(jnp.bfloat16)
    return (layer_out, new_kv)


def solution(mesh):
    return jax.shard_map(
        local,
        mesh=mesh,
        in_specs=(
            P(("req", "head"), None),
            P(),
            P(None, "head", None),
            P("head", None),
            P("req", "head", None, None),
            P("req"),
            P(),
            P(),
            P(("req", "head"), None),
            P("req", None, None),
            P("req", None, None),
        ),
        out_specs=(P(("req", "head"), None), P("req", "head", None)),
        check_vma=False,
    )
```

profile of v0, /device:TPU:0, one launch (start us, length us, event | category | flops | bytes accessed | tf_op | source)
XLA Modules:
  0.0 164.2 jit_solution(350964640558112470)
XLA Ops:
  7.2 0.8 convert_element_type.116
  8.0 0.7 iota_compare_fusion.2
  8.8 1.0 fusion.46
  9.8 0.7 convert_element_type.114
  10.5 1.0 fusion.48
  11.5 7.9 %all_gather.3 = bf16[128,1536]{1,0:T(8,128)(2,1)S(1)} all-gather(bf16[32,1536]{1,0:T(8,128)(2,1)S(1)} %fusion.48), channel_id=1, replica_groups=mesh['req'=8,'head'=4] {'head'}, dimensions={0}, use_global_device_ids=true | all-gather | bytes 491520 | tf_op jit(solution)/shard_map/all_gather | solution.py:93
  19.4 0.7 fusion.42
  20.1 0.1 multiply_cosine_fusion
  20.4 0.8 copy.89
  21.1 0.2 copy.81
  21.3 12.0 %fusion.69 = (f32[128,2,3]{2,1,0:T(2,128)}, f32[128,2,3,192]{3,2,1,0:T(4,128)S(1)}) fusion(bf16[128,2,3,64]{3,2,1,0:T(4,128)(2,1)S(1)} %copy.81, bf16[128,2,192,128]{3,2,1,0:T(8,128)(2,1)} %param.15, pred[128,192]{1,0:T(8,128)(4,1)S(1)} %iota_compare_fusion.2), kind=kOutput, calls=%fused_computation.101 | convolution fusion | flops 19315968 | bytes 13298688 | tf_op jit(solution)/shard_map/rkgd,rkld->rkgl/dot_general | solution.py:54
  33.3 1.1 copy.85
  34.4 0.2 copy.86
  34.6 0.8 fusion.35
  35.6 0.8 copy.88
  36.4 0.8 copy.91
  37.2 9.9 %fusion.30 = bf16[128,2,3,64]{3,2,1,0:T(4,128)(2,1)} fusion(bf16[128,2,192,128]{3,2,1,0:T(8,128)(2,1)} %param.15, f32[128,2,3,192]{3,2,1,0:T(4,128)} %copy-done.3, f32[128,2,3]{2,1,0:T(2,128)S(1)} %copy.86, pred[128,192]{1,0:T(8,128)(4,1)S(1)} %iota_compare_fusion.2, f32[128,2,3]{2,1,0:T(2,128)} %copy.91, f32[128,2,64]{2,1,0:T(2,128)} %copy.89, ...), kind=kOutput, calls=%fused_computation.22 | convolution fusion | flops 19513344 | bytes 13370368 | tf_op jit(solution)/shard_map/rkgl,rkld->rkgd/dot_general | solution.py:66
  47.1 1.1 copy.92
  48.2 1.1 convolution_convert_fusion.1
  49.5 0.1 reshape.238
  49.6 0.1 eq.39
  49.7 0.6 reduce-window.6
  50.3 0.2 slice_reduce_fusion
  50.5 0.1 fusion.58
  50.6 20.7 %reduce-scatter.2.cloned.1.call-done = bf16[32,1536]{1,0:T(8,128)(2,1)} async-done(((bf16[128,1536]{1,0:T(8,128)(2,1)}), bf16[32,1536]{1,0:T(8,128)(2,1)}) %reduce-scatter.2.cloned.1.call-update) | async-done | bytes 98320 | tf_op jit(solution)/shard_map/reduce_scatter | solution.py:102
  71.3 1.0 fusion.50
  72.3 1.0 fusion.52
  73.3 0.5 convolution_convert_fusion
  73.9 1.2 reshape.241
  75.1 5.5 %all-to-all-start = ((bf16[8,3,12,1536]{3,2,1,0:T(8,128)(2,1)}), bf16[8,3,12,1536]{3,2,1,0:T(8,128)(2,1)S(1)}, u32[]{:S(2)}, u32[]{:S(2)}) async-start(bf16[8,3,12,1536]{3,2,1,0:T(8,128)(2,1)} %reshape.241), calls=%async_computation.1 | async-start | bytes 2359296 | tf_op jit(solution)/shard_map/all_to_all | solution.py:130
  80.7 0.1 mul.257
  80.8 28.4 %all-to-all-done = bf16[8,3,12,1536]{3,2,1,0:T(8,128)(2,1)S(1)} async-done(((bf16[8,3,12,1536]{3,2,1,0:T(8,128)(2,1)}), bf16[8,3,12,1536]{3,2,1,0:T(8,128)(2,1)S(1)}, u32[]{:S(2)}, u32[]{:S(2)}) %all-to-all-start) | async-done | bytes 884768 | tf_op jit(solution)/shard_map/all_to_all | solution.py:130
  109.1 5.1 %fusion.14 = f32[8,3,12,1024]{3,2,0,1:T(8,128)S(1)} fusion(bf16[3,1536,1024]{2,1,0:T(8,128)(2,1)} %param.20, bf16[8,3,12,1536]{3,2,1,0:T(8,128)(2,1)S(1)} %all-to-all-done), kind=kOutput, calls=%fused_computation.15 | convolution fusion | flops 905969664 | bytes 11501568 | tf_op jit(solution)/shard_map/sjcd,jdf->sjcf/dot_general | solution.py:128
  114.2 3.2 %fusion.11 = bf16[8,3,12,1536]{3,2,0,1:T(8,128)(2,1)S(1)} fusion(bf16[3,512,1536]{2,1,0:T(8,128)(2,1)} %param.21, f32[8,3,12,1024]{3,2,0,1:T(8,128)S(1)} %fusion.14), kind=kOutput, calls=%fused_computation.12 | convolution fusion | flops 454311936 | bytes 6782976 | tf_op jit(solution)/shard_map/sjcf,jfd->sjcd/dot_general | solution.py:135
  117.5 1.1 copy.101
  118.6 4.2 %all-to-all-start.1 = ((bf16[8,3,12,1536]{3,2,1,0:T(8,128)(2,1)}), bf16[8,3,12,1536]{3,2,1,0:T(8,128)(2,1)}, u32[]{:S(2)}, u32[]{:S(2)}) async-start(bf16[8,3,12,1536]{3,2,1,0:T(8,128)(2,1)} %copy.101), calls=%async_computation.2 | async-start | bytes 2359296 | tf_op jit(solution)/shard_map/all_to_all | solution.py:138
  122.9 0.1 reshape.251
  123.0 0.8 copy.102
  123.8 0.1 fusion.70
  123.9 2.0 %gather_fusion.1 = f32[256]{0:T(256)S(1)} fusion(f32[32,24]{0,1:T(8,128)S(1)} %fusion.70, s32[256]{0:T(256)S(1)} %reshape.251), kind=kCustom, calls=%fused_computation.1 | custom fusion | bytes 4096 | tf_op jit(solution)/shard_map/jit(take_along_axis)/gather | solution.py:111
  126.0 0.1 fusion.68
  126.1 0.2 fusion.63
  126.3 0.1 fusion.62
  126.4 24.8 %all-to-all-done.1 = bf16[8,3,12,1536]{3,2,1,0:T(8,128)(2,1)} async-done(((bf16[8,3,12,1536]{3,2,1,0:T(8,128)(2,1)}), bf16[8,3,12,1536]{3,2,1,0:T(8,128)(2,1)}, u32[]{:S(2)}, u32[]{:S(2)}) %all-to-all-start.1) | async-done | bytes 884768 | tf_op jit(solution)/shard_map/all_to_all | solution.py:138
  151.2 1.3 reshape.242
  152.5 2.1 %gather_fusion = bf16[256,1536]{1,0:T(8,128)(2,1)} fusion(bf16[288,1536]{1,0:T(8,128)(2,1)S(1)} %reshape.242, s32[1024]{0:T(1024)S(1)} %pad_clamp_fusion), kind=kCustom, calls=%fused_computation | custom fusion | bytes 1573888 | tf_op jit(solution)/shard_map/jit(_take)/gather | solution.py:139
  154.7 2.0 %multiply_reduce_fusion = f32[32,1536]{1,0:T(8,128)S(1)} fusion(bf16[256,1536]{1,0:T(8,128)(2,1)} %gather_fusion, f32[32,8]{1,0:T(8,128)S(1)} %fusion.62, pred[32,8]{1,0:T(8,128)(4,1)S(1)} %compare_and_fusion), kind=kLoop, calls=%fused_computation.14 | loop fusion | flops 1523712 | bytes 984320 | tf_op jit(solution)/shard_map/reduce_sum | solution.py:142
  156.7 0.7 fusion.53
  (44 shorter events, 0.7 us)
Async XLA Ops:
  7.2 12.3 %copy-start = (bf16[1536,2,320]{0,2,1:T(8,128)(2,1)S(1)}, bf16[1536,2,320]{0,2,1:T(8,128)(2,1)}, u32[]{:S(2)}) copy-start(bf16[1536,2,320]{0,2,1:T(8,128)(2,1)} %param.13) | copy-start | bytes 5898244
  7.2 64.1 %reduce-scatter.2.cloned.1.call-start = ((), (), s32[]{:S(2)}) async-start(), calls=%async_computation.3 | async-start | bytes 491520 | tf_op jit(solution)/shard_map/reduce_scatter | solution.py:102
  33.3 3.0 %copy-start.3 = (f32[128,2,3,192]{3,2,1,0:T(4,128)}, f32[128,2,3,192]{3,2,1,0:T(4,128)S(1)}, u32[]{:S(2)}) copy-start(f32[128,2,3,192]{3,2,1,0:T(4,128)S(1)} %get-tuple-element.21) | copy-start | bytes 1769476
  37.2 11.1 %copy-start.2 = (bf16[384,1536]{1,0:T(8,128)(2,1)S(1)}, bf16[384,1536]{1,0:T(8,128)(2,1)}, u32[]{:S(2)}) copy-start(bf16[384,1536]{1,0:T(8,128)(2,1)} %param.14) | copy-start | bytes 3538948
  47.1 2.3 %copy-start.6 = (s32[32,8]{0,1:T(8,128)S(1)}, s32[32,8]{0,1:T(8,128)}, u32[]{:S(2)}) copy-start(s32[32,8]{0,1:T(8,128)} %param.19) | copy-start | bytes 3076
  47.1 2.6 %copy-start.7 = (bf16[1536]{0:T(1024)(128)(2,1)S(1)}, bf16[1536]{0:T(1024)(128)(2,1)}, u32[]{:S(2)}) copy-start(bf16[1536]{0:T(1024)(128)(2,1)} %param.17) | copy-start | bytes 9220
  47.1 24.2 %copy-start.1 = (bf16[32,1536]{1,0:T(8,128)(2,1)S(1)}, bf16[32,1536]{1,0:T(8,128)(2,1)}, u32[]{:S(2)}) copy-start(bf16[32,1536]{1,0:T(8,128)(2,1)} %param.11) | copy-start | bytes 294916
  75.1 34.1 %all-to-all-start = ((bf16[8,3,12,1536]{3,2,1,0:T(8,128)(2,1)}), bf16[8,3,12,1536]{3,2,1,0:T(8,128)(2,1)S(1)}, u32[]{:S(2)}, u32[]{:S(2)}) async-start(bf16[8,3,12,1536]{3,2,1,0:T(8,128)(2,1)} %reshape.241), calls=%async_computation.1 | async-start | bytes 2359296 | tf_op jit(solution)/shard_map/all_to_all | solution.py:130
  117.4 6.3 %copy-start.5 = (bf16[1536,24]{0,1:T(8,128)(2,1)S(1)}, bf16[1536,24]{0,1:T(8,128)(2,1)}, u32[]{:S(2)}) copy-start(bf16[1536,24]{0,1:T(8,128)(2,1)} %param.18) | copy-start | bytes 221188
  118.6 32.6 %all-to-all-start.1 = ((bf16[8,3,12,1536]{3,2,1,0:T(8,128)(2,1)}), bf16[8,3,12,1536]{3,2,1,0:T(8,128)(2,1)}, u32[]{:S(2)}, u32[]{:S(2)}) async-start(bf16[8,3,12,1536]{3,2,1,0:T(8,128)(2,1)} %copy.101), calls=%async_computation.2 | async-start | bytes 2359296 | tf_op jit(solution)/shard_map/all_to_all | solution.py:138
  152.5 4.1 %copy-start.4 = (bf16[32,1536]{1,0:T(8,128)(2,1)S(1)}, bf16[32,1536]{1,0:T(8,128)(2,1)}, u32[]{:S(2)}) copy-start(bf16[32,1536]{1,0:T(8,128)(2,1)} %reduce-scatter.2.cloned.1.call-done) | copy-start | bytes 294916
Sparse Core Ops, SparseCore 0:
  49.5 21.7 reduce-scatter.1
where the time goes:
time: 165 us; the launch traced here: 164 us
  waiting for transfers between devices  73.8 us (45%)
  matrix products  32.6 us (20%)
  local copies, waits for them, and re-layouts  14.4 us (9%)
  between operations  14.3 us (9%)
  other arithmetic  11.2 us (7%)
  starting transfers between devices  9.81 us (6%)
  blocking collectives  7.94 us (5%)
    all_to_all x1, waiting for transfers between devices, local(): lax.all_to_all(outgoing, 'req', split_axis=0, concat_axis=0, tiled=True)  28.4 us
    all_to_all x1, waiting for transfers between devices, local(): lax.all_to_all(result, 'req', split_axis=0, concat_axis=0, tiled=True)  24.8 us
    reduce_scatter x1, waiting for transfers between devices, local(): lax.psum_scatter(jnp.dot(attn_heads, w_out, preferred_element_type=jnp.fl...  20.7 us
    dot_general x1, matrix products, attend_full(): jnp.einsum('rkgd,rkld->rkgl', queries, cache[..., :HD], preferred_element...  12 us
    dot_general x1, matrix products, attend_full(): jnp.einsum('rkgl,rkld->rkgd', probabilities, cache[..., HD:], preferred_e...  9.91 us
    all_gather x1, blocking collectives, local(): lax.all_gather(normed, 'head', axis=0, tiled=True)  7.94 us
    all_to_all x1, starting transfers between devices, local(): lax.all_to_all(outgoing, 'req', split_axis=0, concat_axis=0, tiled=True)  5.52 us
    dot_general x1, matrix products, local(): jnp.einsum('sjcd,jdf->sjcf', lax.all_to_all(outgoing, 'req', split_axis=0...  5.07 us
  transfers between devices with their start and end apart: 3, of which 3 were waited for; matrix products, arithmetic and copies ran while one was open for 3% of the time, Pallas kernels for 0%

commit v1 on v0

--- a/solution.py
+++ b/solution.py
@@ -10,6 +10,28 @@
 F = 512
 EPSILON = 1e-06
 THETA = 10000.0
+
+
+def in_order(blocks, dim):
+    shape = list(blocks.shape[1:])
+    shape[dim] *= blocks.shape[0]
+    return jnp.moveaxis(blocks, 0, dim).reshape(shape)
+
+
+def grow_blocks(value, axis):
+    size = lax.axis_size(axis)
+    blocks = value[None]
+    for level in range(size.bit_length() - 1):
+        stride = 1 << level
+        received = lax.ppermute(blocks, axis, [(i, i ^ stride) for i in range(size)])
+        both = jnp.stack([blocks, received])
+        upper = lax.axis_index(axis) >> level & 1
+        blocks = jnp.where(upper == 0, both, both[::-1]).reshape(-1, *value.shape)
+    return blocks
+
+
+def doubled_up(value, axis, dim):
+    return in_order(grow_blocks(value, axis), dim)
 
 
 def rms_scale(values, gain):
@@ -90,9 +112,7 @@
     normed = rms_scale(residual_in, attn_gain)
     flat_weight = w_qkv.reshape(D, kv_local * (group + 2) * HD)
     projected = jnp.dot(
-        lax.all_gather(normed, "head", axis=0, tiled=True),
-        flat_weight,
-        preferred_element_type=jnp.float32,
+        doubled_up(normed, "head", 0), flat_weight, preferred_element_type=jnp.float32
     )
     queries, new_keys, new_values = project_heads(projected, lengths, group, HD)
     new_kv = jnp.concatenate([new_keys, new_values], axis=-1)

time: 165 us -> 166 us (level)
  blocking collectives: 7.94 us -> 0 us
  waiting for transfers between devices: 73.8 us -> 79 us
  starting transfers between devices: 9.81 us -> 13.3 us
    all_gather x1 -> x0, blocking collectives: 7.94 us -> none  [local(): lax.all_gather(normed, 'head', axis=0, tiled=True)]
    ppermute x0 -> x2, waiting for transfers between devices: none -> 4.59 us  [grow_blocks(): lax.ppermute(blocks, axis, [(i, i ^ stride) for i in range(size)])]
    ppermute x0 -> x2, starting transfers between devices: none -> 3.45 us  [grow_blocks(): lax.ppermute(blocks, axis, [(i, i ^ stride) for i in range(size)])]
  transfers between devices with their start and end apart: 3 -> 5, of which waited for: 3 -> 5; matrix products, arithmetic and copies ran while one was open for 3% -> 4% of each run, Pallas kernels for 0% -> 0%
where the time goes in v1:
time: 166 us; the launch traced here: 165 us
  waiting for transfers between devices  79 us (48%)
  matrix products  32.6 us (20%)
  local copies, waits for them, and re-layouts  14.4 us (9%)
  between operations  14.4 us (9%)
  starting transfers between devices  13.3 us (8%)
  other arithmetic  11.4 us (7%)
    all_to_all x1, waiting for transfers between devices, local(): lax.all_to_all(outgoing, 'req', split_axis=0, concat_axis=0, tiled=True)  28.4 us
    all_to_all x1, waiting for transfers between devices, local(): lax.all_to_all(result, 'req', split_axis=0, concat_axis=0, tiled=True)  24.7 us
    reduce_scatter x1, waiting for transfers between devices, local(): lax.psum_scatter(jnp.dot(attn_heads, w_out, preferred_element_type=jnp.fl...  21.2 us
    dot_general x1, matrix products, attend_full(): jnp.einsum('rkgd,rkld->rkgl', queries, cache[..., :HD], preferred_element...  12 us
    dot_general x1, matrix products, attend_full(): jnp.einsum('rkgl,rkld->rkgd', probabilities, cache[..., HD:], preferred_e...  9.91 us
    all_to_all x1, starting transfers between devices, local(): lax.all_to_all(outgoing, 'req', split_axis=0, concat_axis=0, tiled=True)  5.52 us
    dot_general x1, matrix products, local(): jnp.einsum('sjcd,jdf->sjcf', lax.all_to_all(outgoing, 'req', split_axis=0...  5.07 us
    ppermute x2, waiting for transfers between devices, grow_blocks(): lax.ppermute(blocks, axis, [(i, i ^ stride) for i in range(size)])  4.59 us
  transfers between devices with their start and end apart: 5, of which 5 were waited for; matrix products, arithmetic and copies ran while one was open for 4% of the time, Pallas kernels for 0%

profile of v1, /device:TPU:0, one launch (start us, length us, event | category | flops | bytes accessed | tf_op | source)
XLA Modules:
  0.0 165.1 jit_solution(1620900940691937217)
XLA Ops:
  7.2 1.2 fusion.44
  8.4 0.7 convert_element_type.114
  9.1 1.0 fusion.61
  10.1 0.5 collective-permute-start
  10.6 0.7 convert_element_type.116
  11.3 0.1 multiply_cosine_fusion
  11.4 0.1 collective-permute-done
  11.6 2.9 %collective-permute-start.1 = (bf16[2,32,1536]{2,1,0:T(8,128)(2,1)S(1)}, bf16[2,32,1536]{2,1,0:T(8,128)(2,1)S(1)}, u32[]{:S(2)}, u32[]{:S(2)}) collective-permute-start(bf16[2,32,1536]{2,1,0:T(8,128)(2,1)S(1)} %get-tuple-element.17), channel_id=1, source_target_pairs={{0,2},{1,3},{2,0},{3,1},{4,6},{5,7},{6,4},{7,5},{8,10},{9,11},{10,... | collective-permute-start | bytes 589832 | tf_op jit(solution)/shard_map/ppermute | solution.py:26
  14.5 0.7 iota_compare_fusion.2
  15.3 4.5 %collective-permute-done.1 = bf16[2,32,1536]{2,1,0:T(8,128)(2,1)S(1)} collective-permute-done((bf16[2,32,1536]{2,1,0:T(8,128)(2,1)S(1)}, bf16[2,32,1536]{2,1,0:T(8,128)(2,1)S(1)}, u32[]{:S(2)}, u32[]{:S(2)}) %collective-permute-start.1) | collective-permute-done | bytes 196640 | tf_op jit(solution)/shard_map/ppermute | solution.py:26
  19.9 0.7 fusion.72
  20.7 0.8 copy.89
  21.5 0.2 copy.81
  21.7 12.0 %fusion.71 = (f32[128,2,3]{2,1,0:T(2,128)}, f32[128,2,3,192]{3,2,1,0:T(4,128)S(1)}) fusion(bf16[128,2,3,64]{3,2,1,0:T(4,128)(2,1)S(1)} %copy.81, bf16[128,2,192,128]{3,2,1,0:T(8,128)(2,1)} %param.15, pred[128,192]{1,0:T(8,128)(4,1)S(1)} %iota_compare_fusion.2), kind=kOutput, calls=%fused_computation.107 | convolution fusion | flops 19315968 | bytes 13298688 | tf_op jit(solution)/shard_map/rkgd,rkld->rkgl/dot_general | solution.py:76
  33.7 1.1 copy.85
  34.7 0.2 copy.86
  34.9 0.8 fusion.35
  35.9 0.8 copy.88
  36.7 0.8 copy.91
  37.5 9.9 %fusion.30 = bf16[128,2,3,64]{3,2,1,0:T(4,128)(2,1)} fusion(bf16[128,2,192,128]{3,2,1,0:T(8,128)(2,1)} %param.15, f32[128,2,3,192]{3,2,1,0:T(4,128)} %copy-done.3, f32[128,2,3]{2,1,0:T(2,128)S(1)} %copy.86, pred[128,192]{1,0:T(8,128)(4,1)S(1)} %iota_compare_fusion.2, f32[128,2,3]{2,1,0:T(2,128)} %copy.91, f32[128,2,64]{2,1,0:T(2,128)} %copy.89, ...), kind=kOutput, calls=%fused_computation.22 | convolution fusion | flops 19513344 | bytes 13370368 | tf_op jit(solution)/shard_map/rkgl,rkld->rkgd/dot_general | solution.py:88
  47.4 1.1 copy.92
  48.5 1.1 convolution_convert_fusion.1
  50.0 0.6 reduce-window.6
  50.6 0.2 slice_reduce_fusion
  50.8 0.1 fusion.58
  50.9 21.2 %reduce-scatter.2.cloned.1.call-done = bf16[32,1536]{1,0:T(8,128)(2,1)} async-done(((bf16[128,1536]{1,0:T(8,128)(2,1)}), bf16[32,1536]{1,0:T(8,128)(2,1)}) %reduce-scatter.2.cloned.1.call-update) | async-done | bytes 98320 | tf_op jit(solution)/shard_map/reduce_scatter | solution.py:122
  72.2 1.0 fusion.48
  73.2 1.0 fusion.50
  74.2 0.5 convolution_convert_fusion
  74.7 1.2 reshape.245
  75.9 5.5 %all-to-all-start = ((bf16[8,3,12,1536]{3,2,1,0:T(8,128)(2,1)}), bf16[8,3,12,1536]{3,2,1,0:T(8,128)(2,1)S(1)}, u32[]{:S(2)}, u32[]{:S(2)}) async-start(bf16[8,3,12,1536]{3,2,1,0:T(8,128)(2,1)} %reshape.245), calls=%async_computation.1 | async-start | bytes 2359296 | tf_op jit(solution)/shard_map/all_to_all | solution.py:150
  81.5 0.1 mul.257
  81.6 28.4 %all-to-all-done = bf16[8,3,12,1536]{3,2,1,0:T(8,128)(2,1)S(1)} async-done(((bf16[8,3,12,1536]{3,2,1,0:T(8,128)(2,1)}), bf16[8,3,12,1536]{3,2,1,0:T(8,128)(2,1)S(1)}, u32[]{:S(2)}, u32[]{:S(2)}) %all-to-all-start) | async-done | bytes 884768 | tf_op jit(solution)/shard_map/all_to_all | solution.py:150
  110.0 5.1 %fusion.14 = f32[8,3,12,1024]{3,2,0,1:T(8,128)S(1)} fusion(bf16[3,1536,1024]{2,1,0:T(8,128)(2,1)} %param.20, bf16[8,3,12,1536]{3,2,1,0:T(8,128)(2,1)S(1)} %all-to-all-done), kind=kOutput, calls=%fused_computation.15 | convolution fusion | flops 905969664 | bytes 11501568 | tf_op jit(solution)/shard_map/sjcd,jdf->sjcf/dot_general | solution.py:148
  115.1 3.2 %fusion.11 = bf16[8,3,12,1536]{3,2,0,1:T(8,128)(2,1)S(1)} fusion(bf16[3,512,1536]{2,1,0:T(8,128)(2,1)} %param.21, f32[8,3,12,1024]{3,2,0,1:T(8,128)S(1)} %fusion.14), kind=kOutput, calls=%fused_computation.12 | convolution fusion | flops 454311936 | bytes 6782976 | tf_op jit(solution)/shard_map/sjcf,jfd->sjcd/dot_general | solution.py:155
  118.3 1.1 copy.101
  119.4 4.2 %all-to-all-start.1 = ((bf16[8,3,12,1536]{3,2,1,0:T(8,128)(2,1)}), bf16[8,3,12,1536]{3,2,1,0:T(8,128)(2,1)}, u32[]{:S(2)}, u32[]{:S(2)}) async-start(bf16[8,3,12,1536]{3,2,1,0:T(8,128)(2,1)} %copy.101), calls=%async_computation.2 | async-start | bytes 2359296 | tf_op jit(solution)/shard_map/all_to_all | solution.py:158
  123.9 0.8 copy.102
  124.6 0.1 fusion.73
  124.8 2.0 %gather_fusion.1 = f32[256]{0:T(256)S(1)} fusion(f32[32,24]{0,1:T(8,128)S(1)} %fusion.73, s32[256]{0:T(256)S(1)} %reshape.255), kind=kCustom, calls=%fused_computation.1 | custom fusion | bytes 4096 | tf_op jit(solution)/shard_map/jit(take_along_axis)/gather | solution.py:131
  126.9 0.1 fusion.70
  127.0 0.2 fusion.65
  127.2 0.1 fusion.64
  127.3 24.7 %all-to-all-done.1 = bf16[8,3,12,1536]{3,2,1,0:T(8,128)(2,1)} async-done(((bf16[8,3,12,1536]{3,2,1,0:T(8,128)(2,1)}), bf16[8,3,12,1536]{3,2,1,0:T(8,128)(2,1)}, u32[]{:S(2)}, u32[]{:S(2)}) %all-to-all-start.1) | async-done | bytes 884768 | tf_op jit(solution)/shard_map/all_to_all | solution.py:158
  152.1 1.3 reshape.246
  153.4 2.1 %gather_fusion = bf16[256,1536]{1,0:T(8,128)(2,1)} fusion(bf16[288,1536]{1,0:T(8,128)(2,1)S(1)} %reshape.246, s32[1024]{0:T(1024)S(1)} %pad_clamp_fusion), kind=kCustom, calls=%fused_computation | custom fusion | bytes 1573888 | tf_op jit(solution)/shard_map/jit(_take)/gather | solution.py:159
  155.5 2.0 %multiply_reduce_fusion = f32[32,1536]{1,0:T(8,128)S(1)} fusion(bf16[256,1536]{1,0:T(8,128)(2,1)} %gather_fusion, f32[32,8]{1,0:T(8,128)S(1)} %fusion.64, pred[32,8]{1,0:T(8,128)(4,1)S(1)} %compare_and_fusion), kind=kLoop, calls=%fused_computation.14 | loop fusion | flops 1523712 | bytes 984320 | tf_op jit(solution)/shard_map/reduce_sum | solution.py:162
  157.5 0.7 fusion.51
  (51 shorter events, 1.1 us)
Async XLA Ops:
  7.2 12.7 %copy-start = (bf16[1536,2,320]{0,2,1:T(8,128)(2,1)S(1)}, bf16[1536,2,320]{0,2,1:T(8,128)(2,1)}, u32[]{:S(2)}) copy-start(bf16[1536,2,320]{0,2,1:T(8,128)(2,1)} %param.13) | copy-start | bytes 5898244
  7.2 65.0 %reduce-scatter.2.cloned.1.call-start = ((), (), s32[]{:S(2)}) async-start(), calls=%async_computation.3 | async-start | bytes 491520 | tf_op jit(solution)/shard_map/reduce_scatter | solution.py:122
  10.1 1.5 collective-permute-start
  11.6 8.2 %collective-permute-start.1 = (bf16[2,32,1536]{2,1,0:T(8,128)(2,1)S(1)}, bf16[2,32,1536]{2,1,0:T(8,128)(2,1)S(1)}, u32[]{:S(2)}, u32[]{:S(2)}) collective-permute-start(bf16[2,32,1536]{2,1,0:T(8,128)(2,1)S(1)} %get-tuple-element.17), channel_id=1, source_target_pairs={{0,2},{1,3},{2,0},{3,1},{4,6},{5,7},{6,4},{7,5},{8,10},{9,11},{10,... | collective-permute-start | bytes 589832 | tf_op jit(solution)/shard_map/ppermute | solution.py:26
  33.6 3.0 %copy-start.3 = (f32[128,2,3,192]{3,2,1,0:T(4,128)}, f32[128,2,3,192]{3,2,1,0:T(4,128)S(1)}, u32[]{:S(2)}) copy-start(f32[128,2,3,192]{3,2,1,0:T(4,128)S(1)} %get-tuple-element.25) | copy-start | bytes 1769476
  37.5 11.1 %copy-start.2 = (bf16[384,1536]{1,0:T(8,128)(2,1)S(1)}, bf16[384,1536]{1,0:T(8,128)(2,1)}, u32[]{:S(2)}) copy-start(bf16[384,1536]{1,0:T(8,128)(2,1)} %param.14) | copy-start | bytes 3538948
  47.4 2.3 %copy-start.6 = (s32[32,8]{0,1:T(8,128)S(1)}, s32[32,8]{0,1:T(8,128)}, u32[]{:S(2)}) copy-start(s32[32,8]{0,1:T(8,128)} %param.19) | copy-start | bytes 3076
  47.4 2.6 %copy-start.7 = (bf16[1536]{0:T(1024)(128)(2,1)S(1)}, bf16[1536]{0:T(1024)(128)(2,1)}, u32[]{:S(2)}) copy-start(bf16[1536]{0:T(1024)(128)(2,1)} %param.17) | copy-start | bytes 9220
  47.4 24.8 %copy-start.1 = (bf16[32,1536]{1,0:T(8,128)(2,1)S(1)}, bf16[32,1536]{1,0:T(8,128)(2,1)}, u32[]{:S(2)}) copy-start(bf16[32,1536]{1,0:T(8,128)(2,1)} %param.11) | copy-start | bytes 294916
  75.9 34.1 %all-to-all-start = ((bf16[8,3,12,1536]{3,2,1,0:T(8,128)(2,1)}), bf16[8,3,12,1536]{3,2,1,0:T(8,128)(2,1)S(1)}, u32[]{:S(2)}, u32[]{:S(2)}) async-start(bf16[8,3,12,1536]{3,2,1,0:T(8,128)(2,1)} %reshape.245), calls=%async_computation.1 | async-start | bytes 2359296 | tf_op jit(solution)/shard_map/all_to_all | solution.py:150
  118.3 6.3 %copy-start.5 = (bf16[1536,24]{0,1:T(8,128)(2,1)S(1)}, bf16[1536,24]{0,1:T(8,128)(2,1)}, u32[]{:S(2)}) copy-start(bf16[1536,24]{0,1:T(8,128)(2,1)} %param.18) | copy-start | bytes 221188
  119.4 32.6 %all-to-all-start.1 = ((bf16[8,3,12,1536]{3,2,1,0:T(8,128)(2,1)}), bf16[8,3,12,1536]{3,2,1,0:T(8,128)(2,1)}, u32[]{:S(2)}, u32[]{:S(2)}) async-start(bf16[8,3,12,1536]{3,2,1,0:T(8,128)(2,1)} %copy.101), calls=%async_computation.2 | async-start | bytes 2359296 | tf_op jit(solution)/shard_map/all_to_all | solution.py:158
  153.4 4.1 %copy-start.4 = (bf16[32,1536]{1,0:T(8,128)(2,1)S(1)}, bf16[32,1536]{1,0:T(8,128)(2,1)}, u32[]{:S(2)}) copy-start(bf16[32,1536]{1,0:T(8,128)(2,1)} %reduce-scatter.2.cloned.1.call-done) | copy-start | bytes 294916
Sparse Core Ops, SparseCore 0:
  49.8 22.2 reduce-scatter.1
